TPU v7x, 32 devices: a whole 2x2x4 slice. The times are simulated.
32 devices in a mesh: wide: 8 (over z, core), narrow: 4 (over y, x).
Axes of the slice: x: 2, y: 2, z: 4, core: 2. Of those that a mesh axis runs over, the one named last changes fastest.
Arguments:
- tokens: bfloat16 [4096, 2048], P('wide'), may hold values from -6 to 6
- attn_gain: bfloat16 [2048], replicated, may hold values from 0.099609375 to 1.8984375
- w_query: bfloat16 [2048, 2048], P(None, 'narrow'), may hold values from -0.125 to 0.125
- w_key: bfloat16 [2048, 512], P(None, 'narrow'), may hold values from -0.125 to 0.125
- w_value: bfloat16 [2048, 512], P(None, 'narrow'), may hold values from -0.125 to 0.125
- w_out: bfloat16 [2048, 2048], P('narrow'), may hold values from -2 to 2
- ffn_gain: bfloat16 [2048], replicated, may hold values from 0.099609375 to 1.8984375
- w_gate: bfloat16 [2048, 8192], P(None, 'narrow'), may hold values from -0.125 to 0.125
- w_up: bfloat16 [2048, 8192], P(None, 'narrow'), may hold values from -0.125 to 0.125
- w_down: bfloat16 [8192, 2048], P('narrow'), may hold values from -0.0625 to 0.0625
- doc_lengths: int32 [12], replicated, may hold values from 1 to 2048, 4096 in all
- cotangent: bfloat16 [4096, 2048], P('wide'), may hold values from -6 to 6
Outputs:
- output: bfloat16 [4096, 2048], P('wide')
- input_grad: bfloat16 [4096, 2048], P('wide')
- grad_attn_gain: float32 [2048], P('wide')
- grad_query: float32 [2048, 2048], P('wide', 'narrow')
- grad_key: float32 [2048, 512], P('wide', 'narrow')
- grad_value: float32 [2048, 512], P('wide', 'narrow')
- grad_out: float32 [2048, 2048], P('narrow', 'wide')
- grad_ffn_gain: float32 [2048], P('wide')
- grad_gate: float32 [2048, 8192], P('wide', 'narrow')
- grad_up: float32 [2048, 8192], P('wide', 'narrow')
- grad_down: float32 [8192, 2048], P('narrow', 'wide')
Inputs may be any that keep to these rules, and one draw needn't show every extreme that they name: `doc_lengths`: the last entry is the padding at the row's end; the longest entry is exactly 2048.
All inputs are finite; a program needn't handle non-finite values.
Results may differ from a plain program's by a relative error of at most 0.02.
Values may be sent and summed in bfloat16 or wider, within the bound.
No kernel may reach another device: no remote copies, remote signals or barrier semaphores. Data moves between devices by JAX's collectives and lax.ppermute only.
A program may use at most 320 MiB of HBM per device.

v0:
```python
import math
import jax
import jax.numpy as jnp
import numpy as np
from jax import lax
from jax.sharding import PartitionSpec as P

HD = 64
QBLK = 512
DOCS = 12
NORM_EPS = 1e-05
MASKED_SCORE = -1e30


def inverse_frequencies(head_size):
    frequency = 1.0 / 500000.0 ** (np.arange(0, head_size, 2) / head_size)
    wavelength = 2 * math.pi / frequency
    smoothing = (8192.0 / wavelength - 1.0) / 3.0
    scaled_freq = np.where(wavelength > 8192.0, frequency / 32.0, frequency)
    middle_band = (wavelength <= 8192.0) & (wavelength >= 2048.0)
    scaled_freq = np.where(
        middle_band, (1 - smoothing) * frequency / 32.0 + smoothing * frequency, scaled_freq
    )
    return scaled_freq.astype(np.float32)


def doc_layout(doc_lengths, index):
    ends = jnp.cumsum(doc_lengths)
    passed = (index[:, None] >= ends[None, :]).astype(jnp.int32)
    segment = jnp.sum(passed, axis=1)
    offset = jnp.sum(passed * doc_lengths[None, :], axis=1)
    position = index - offset
    valid = index < ends[DOCS - 2]
    return (segment, position, valid)


def rotate(values, position, heads, direction):
    angle = position.astype(jnp.float32)[:, None] * jnp.asarray(inverse_frequencies(HD))[None, :]
    cosine = jnp.cos(angle)[:, None, :]
    sine = direction * jnp.sin(angle)[:, None, :]
    shaped = values.reshape(values.shape[0], heads, 2, HD // 2)
    first = shaped[:, :, 0]
    second = shaped[:, :, 1]
    return jnp.stack(
        [first * cosine - second * sine, second * cosine + first * sine], axis=2
    ).reshape(values.shape)


def contract_rows(left, right):
    return lax.dot_general(
        left, right, (((0,), (0,)), ((), ())), preferred_element_type=jnp.float32
    )


def contract_cols(left, right):
    return lax.dot_general(
        left, right, (((1,), (1,)), ((), ())), preferred_element_type=jnp.float32
    )


def head_scores(query_head, key_head, allowed):
    raw_scores = contract_cols(query_head, key_head)
    return jnp.where(allowed, raw_scores / math.sqrt(HD), MASKED_SCORE)


def norm_back(grad_normed, gain, values, inverse):
    scaled = grad_normed * gain
    return inverse * scaled - values * inverse**3 * jnp.mean(
        scaled * values, axis=-1, keepdims=True
    )


def body(
    tokens,
    attn_gain,
    w_query,
    w_key,
    w_value,
    w_out,
    ffn_gain,
    w_gate,
    w_up,
    w_down,
    doc_lengths,
    cotangent,
):
    rows = tokens.shape[0]
    total = rows * lax.axis_size("wide")
    heads = w_query.shape[1] // HD
    kv_heads = w_key.shape[1] // HD
    group = heads // kv_heads
    blocks = rows // QBLK
    local_index = lax.axis_index("wide") * rows + jnp.arange(rows, dtype=jnp.int32)
    segment, position, valid = doc_layout(doc_lengths, local_index)
    key_index = jnp.arange(total, dtype=jnp.int32)
    key_layout = doc_layout(doc_lengths, key_index)
    key_segment = key_layout[0]
    inputs = tokens.astype(jnp.float32)
    gain_one = attn_gain.astype(jnp.float32)
    gain_two = ffn_gain.astype(jnp.float32)
    inv_one = lax.rsqrt(jnp.mean(inputs * inputs, axis=-1, keepdims=True) + NORM_EPS)
    normed = (inputs * inv_one * gain_one).astype(jnp.bfloat16)
    query = jnp.dot(normed, w_query, preferred_element_type=jnp.float32)
    keys = jnp.dot(normed, w_key, preferred_element_type=jnp.float32)
    values = jnp.dot(normed, w_value, preferred_element_type=jnp.float32).astype(jnp.bfloat16)
    query_r = rotate(query, position, heads, 1.0).astype(jnp.bfloat16)
    keys_r = rotate(keys, position, kv_heads, 1.0).astype(jnp.bfloat16)
    packed = jnp.concatenate([keys_r, values], axis=1)
    gathered = lax.all_gather(packed, "wide", axis=0, tiled=True)
    width = kv_heads * HD
    all_keys = gathered[:, :width]
    all_values = gathered[:, width:]

    def block_mask(segment_block, index_block):
        return (segment_block[:, None] == key_segment[None, :]) & (
            index_block[:, None] >= key_index[None, :]
        )

    def attend(block_in):
        query_block, segment_block, index_block = block_in
        allowed = block_mask(segment_block, index_block)
        outputs = []
        totals = []
        for head in range(heads):
            column = head // group * HD
            scores = head_scores(
                query_block[:, head * HD : (head + 1) * HD],
                all_keys[:, column : column + HD],
                allowed,
            )
            row_max = jnp.max(scores, axis=1, keepdims=True)
            exponent = jnp.exp(scores - row_max)
            row_sum = jnp.sum(exponent, axis=1, keepdims=True)
            probs = (exponent / row_sum).astype(jnp.bfloat16)
            outputs.append(
                jnp.dot(
                    probs, all_values[:, column : column + HD], preferred_element_type=jnp.float32
                )
            )
            totals.append(row_max[:, 0] + jnp.log(row_sum[:, 0]))
        return (jnp.concatenate(outputs, axis=1), jnp.stack(totals, axis=1))

    query_blocks = query_r.reshape(blocks, QBLK, heads * HD)
    segment_blocks = segment.reshape(blocks, QBLK)
    index_blocks = local_index.reshape(blocks, QBLK)
    attended, log_sums = lax.map(attend, (query_blocks, segment_blocks, index_blocks))
    valid_rows = valid[:, None]
    mixed = jnp.where(valid_rows, attended.reshape(rows, heads * HD), 0.0).astype(jnp.bfloat16)
    attn_part = jnp.dot(mixed, w_out, preferred_element_type=jnp.float32)
    hidden_one = inputs + lax.psum(attn_part, "narrow")
    inv_two = lax.rsqrt(jnp.mean(hidden_one * hidden_one, axis=-1, keepdims=True) + NORM_EPS)
    normed_two = (hidden_one * inv_two * gain_two).astype(jnp.bfloat16)
    gate = jnp.dot(normed_two, w_gate, preferred_element_type=jnp.float32)
    up_proj = jnp.dot(normed_two, w_up, preferred_element_type=jnp.float32)
    sigmoid_gate = jax.nn.sigmoid(gate)
    silu_gate = gate * sigmoid_gate
    activ = (silu_gate * up_proj).astype(jnp.bfloat16)
    ffn_part = jnp.dot(activ, w_down, preferred_element_type=jnp.float32)
    grad_down = contract_rows(activ, cotangent)
    d_activ = contract_cols(cotangent, w_down)
    d_gate = (d_activ * up_proj * sigmoid_gate * (1.0 + gate * (1.0 - sigmoid_gate))).astype(
        jnp.bfloat16
    )
    d_up = (d_activ * silu_gate).astype(jnp.bfloat16)
    grad_gate = contract_rows(normed_two, d_gate)
    grad_up = contract_rows(normed_two, d_up)
    norm_two_part = contract_cols(d_gate, w_gate) + contract_cols(d_up, w_up)
    output = (
        hidden_one + lax.psum(ffn_part.astype(jnp.bfloat16), "narrow").astype(jnp.float32)
    ).astype(jnp.bfloat16)
    d_norm_two = lax.psum(norm_two_part.astype(jnp.bfloat16), "narrow").astype(jnp.float32)
    grad_ffn_gain = jnp.sum(d_norm_two * hidden_one * inv_two, axis=0)
    d_hidden = cotangent.astype(jnp.float32) + norm_back(d_norm_two, gain_two, hidden_one, inv_two)
    d_hidden_b = d_hidden.astype(jnp.bfloat16)
    grad_out = contract_rows(mixed, d_hidden_b)
    d_mixed = jnp.where(
        valid_rows,
        contract_cols(d_hidden_b, w_out).astype(jnp.bfloat16),
        jnp.zeros((), jnp.bfloat16),
    )

    def attend_back(carry, block_in):
        query_block, grad_block, lse_block, segment_block, index_block = block_in
        allowed = block_mask(segment_block, index_block)
        query_grads = []
        key_terms = [None] * kv_heads
        value_terms = [None] * kv_heads
        for head in range(heads):
            kv_index = head // group
            column = kv_index * HD
            query_head = query_block[:, head * HD : (head + 1) * HD]
            grad_head = grad_block[:, head * HD : (head + 1) * HD]
            key_head = all_keys[:, column : column + HD]
            value_head = all_values[:, column : column + HD]
            scores = head_scores(query_head, key_head, allowed)
            probs = jnp.where(allowed, jnp.exp(scores - lse_block[:, head : head + 1]), 0.0)
            prob_grad = contract_cols(grad_head, value_head)
            delta = jnp.sum(probs * prob_grad, axis=1, keepdims=True)
            d_scores = (probs * (prob_grad - delta)).astype(jnp.bfloat16)
            query_grads.append(
                jnp.dot(d_scores, key_head, preferred_element_type=jnp.float32) / math.sqrt(HD)
            )
            key_term = contract_rows(d_scores, query_head) / math.sqrt(HD)
            value_term = contract_rows(probs.astype(jnp.bfloat16), grad_head)
            if key_terms[kv_index] is None:
                key_terms[kv_index] = key_term
                value_terms[kv_index] = value_term
            else:
                key_terms[kv_index] = key_terms[kv_index] + key_term
                value_terms[kv_index] = value_terms[kv_index] + value_term
        update = jnp.concatenate(key_terms + value_terms, axis=1)
        return (carry + update, jnp.concatenate(query_grads, axis=1))

    start_terms = jnp.zeros((total, 2 * width), jnp.float32)
    grad_blocks = d_mixed.reshape(blocks, QBLK, heads * HD)
    kv_terms, query_grad_blocks = lax.scan(
        attend_back,
        start_terms,
        (query_blocks, grad_blocks, log_sums, segment_blocks, index_blocks),
    )
    d_kv = lax.psum_scatter(
        kv_terms.astype(jnp.bfloat16), "wide", scatter_dimension=0, tiled=True
    ).astype(jnp.float32)
    d_query = rotate(query_grad_blocks.reshape(rows, heads * HD), position, heads, -1.0).astype(
        jnp.bfloat16
    )
    d_keys = rotate(d_kv[:, :width], position, kv_heads, -1.0).astype(jnp.bfloat16)
    d_values = d_kv[:, width:].astype(jnp.bfloat16)
    grad_query = contract_rows(normed, d_query)
    grad_key = contract_rows(normed, d_keys)
    grad_value = contract_rows(normed, d_values)
    norm_one_part = (
        contract_cols(d_query, w_query)
        + contract_cols(d_keys, w_key)
        + contract_cols(d_values, w_value)
    )
    d_norm_one = lax.psum(norm_one_part.astype(jnp.bfloat16), "narrow").astype(jnp.float32)
    grad_attn_gain = jnp.sum(d_norm_one * inputs * inv_one, axis=0)
    input_grad = (d_hidden + norm_back(d_norm_one, gain_one, inputs, inv_one)).astype(jnp.bfloat16)
    summed = (
        lax.psum_scatter(
            grad_attn_gain.astype(jnp.bfloat16), "wide", scatter_dimension=0, tiled=True
        ).astype(jnp.float32),
        lax.psum_scatter(
            grad_query.astype(jnp.bfloat16), "wide", scatter_dimension=0, tiled=True
        ).astype(jnp.float32),
        lax.psum_scatter(
            grad_key.astype(jnp.bfloat16), "wide", scatter_dimension=0, tiled=True
        ).astype(jnp.float32),
        lax.psum_scatter(
            grad_value.astype(jnp.bfloat16), "wide", scatter_dimension=0, tiled=True
        ).astype(jnp.float32),
        lax.psum_scatter(
            grad_out.astype(jnp.bfloat16), "wide", scatter_dimension=1, tiled=True
        ).astype(jnp.float32),
        lax.psum_scatter(
            grad_ffn_gain.astype(jnp.bfloat16), "wide", scatter_dimension=0, tiled=True
        ).astype(jnp.float32),
        lax.psum_scatter(
            grad_gate.astype(jnp.bfloat16), "wide", scatter_dimension=0, tiled=True
        ).astype(jnp.float32),
        lax.psum_scatter(
            grad_up.astype(jnp.bfloat16), "wide", scatter_dimension=0, tiled=True
        ).astype(jnp.float32),
        lax.psum_scatter(
            grad_down.astype(jnp.bfloat16), "wide", scatter_dimension=1, tiled=True
        ).astype(jnp.float32),
    )
    gain_attn = summed[0]
    gain_ffn = summed[5]
    return (
        output,
        input_grad,
        gain_attn,
        summed[1],
        summed[2],
        summed[3],
        summed[4],
        gain_ffn,
        summed[6],
        summed[7],
        summed[8],
    )


def solution(mesh):
    in_specs = (
        P("wide", None),
        P(),
        P(None, "narrow"),
        P(None, "narrow"),
        P(None, "narrow"),
        P("narrow", None),
        P(),
        P(None, "narrow"),
        P(None, "narrow"),
        P("narrow", None),
        P(),
        P("wide", None),
    )
    out_specs = (
        P("wide", None),
        P("wide", None),
        P("wide"),
        P("wide", "narrow"),
        P("wide", "narrow"),
        P("wide", "narrow"),
        P("narrow", "wide"),
        P("wide"),
        P("wide", "narrow"),
        P("wide", "narrow"),
        P("narrow", "wide"),
    )
    return jax.shard_map(body, mesh=mesh, in_specs=in_specs, out_specs=out_specs, check_vma=False)
```

profile of v0, /device:TPU:0, one launch (start us, length us, event | category | flops | bytes accessed | tf_op | source)
XLA Modules:
  0.0 1095.4 jit_solution(12022537940424208202)
XLA Ops:
  24.1 25.7 %all-gather.2.cloned.1.call-done = bf16[4096,256]{0,1:T(8,128)(2,1)} async-done(((bf16[512,256]{0,1:T(8,128)(2,1)}), bf16[4096,256]{0,1:T(8,128)(2,1)}) %all-gather.2.cloned.1.call-update) | async-done | bytes 2097168 | tf_op jit(solution)/shard_map/all_gather | solution.py:109
  96.0 7.2 fusion.169
  103.1 4.8 fusion.1
  107.9 5.0 fusion.60
  116.7 5.4 fusion.57
  134.7 103.2 %all-reduce.8.cloned.1.call-done = f32[512,2048]{1,0:T(8,128)} async-done(((f32[512,2048]{1,0:T(8,128)}), f32[512,2048]{1,0:T(8,128)}) %all-reduce.8.cloned.1.call-update) | async-done | bytes 4194320 | tf_op jit(solution)/shard_map/psum | solution.py:150
  241.9 9.3 fusion.178
  251.2 6.3 fusion.177
  257.5 12.0 %multiply_convert_fusion.8 = (bf16[512,2048]{1,0:T(8,128)(2,1)}, bf16[512,2048]{1,0:T(8,128)(2,1)}, bf16[512,2048]{1,0:T(8,128)(2,1)}) fusion(f32[512,2048]{1,0:T(8,128)} %fusion.177, f32[512,2048]{1,0:T(8,128)S(1)} %fusion.178, bf16[512,2048]{1,0:T(8,128)(2,1)S(1)} %copy-done.36, bf16[2048,2048]{1,0:T(8,128)(2,1)} %param.25), kind=kOutput, calls=%fused_computation.118 | convolution fusion | flops 4310695936 | bytes 25165824 | tf_op jit(solution)/shard_map/dot_general | solution.py:56
  269.5 7.8 fusion.179
  277.3 9.4 add_convert_fusion.1
  287.2 69.3 %all-reduce.10.cloned.1.call-done = bf16[512,2048]{1,0:T(8,128)(2,1)} async-done(((bf16[512,2048]{1,0:T(8,128)(2,1)}), bf16[512,2048]{1,0:T(8,128)(2,1)}) %all-reduce.10.cloned.1.call-update) | async-done | bytes 2097168 | tf_op jit(solution)/shard_map/psum | solution.py:171
  356.5 4.9 fusion.25
  399.6 4.9 fusion.94
  415.0 26.5 %multiply_reduce_fusion = (f32[512]{0:T(512)S(1)}, f32[512]{0:T(512)S(1)}, f32[512]{0:T(512)S(1)}, f32[512]{0:T(512)S(1)}, f32[512]{0:T(512)S(1)}, /*index=5*/f32[512,4096]{1,0:T(8,128)}) fusion(f32[512,4096]{1,0:T(8,128)} %copy-done.7, f32[512]{0:T(512)S(1)} %log_add_fusion, s32[512]{0:T(512)S(1)} %iota_add_fusion, s32[4096]{0:T(1024)S(1)} %convert_reduce_fusion, ...), kind=kOutput, calls=%fused_computation.7 | convolution fusion | flops 316667392 | bytes 84516864 | tf_op jit(solution)/shard_map/while/body/eval_jaxpr/dot_general | solution.py:56
  441.5 25.5 %multiply_reduce_fusion.1 = (f32[512]{0:T(512)S(1)}, f32[512]{0:T(512)S(1)}, f32[512]{0:T(512)S(1)}, bf16[512,4096]{1,0:T(8,128)(2,1)}, f32[512,4096]{1,0:T(8,128)}) fusion(f32[512,4096]{1,0:T(8,128)} %copy-done.4, f32[512]{0:T(512)S(1)} %get-tuple-element.145, s32[512]{0:T(512)S(1)} %iota_add_fusion, s32[4096]{0:T(1024)S(1)} %convert_reduce_fusion, ...), kind=kOutput, calls=%fused_computation.10 | convolution fusion | flops 310376960 | bytes 71929856 | tf_op jit(solution)/shard_map/while/body/eval_jaxpr/dot_general | solution.py:56
  467.0 21.2 %multiply_convert_fusion.2 = (bf16[512,4096]{1,0:T(8,128)(2,1)}, bf16[512,4096]{1,0:T(8,128)(2,1)}, bf16[512,4096]{1,0:T(8,128)(2,1)S(1)}) fusion(f32[512,4096]{1,0:T(8,128)} %fusion.78, f32[512]{0:T(512)S(1)} %get-tuple-element.88, f32[512,4096]{1,0:T(8,128)} %copy-done.8, f32[512]{0:T(512)S(1)} %get-tuple-element.146, s32[512]{0:T(512)S(1)} %iota_add_fusion, ...), kind=kLoop, calls=%fused_computation.12 | loop fusion | flops 37748736 | bytes 62947328 | tf_op jit(solution)/shard_map/while/body/eval_jaxpr/convert_element_type | solution.py:199
  492.1 27.0 %multiply_convert_fusion.1 = (bf16[512,4096]{1,0:T(8,128)(2,1)}, bf16[512,4096]{1,0:T(8,128)(2,1)}, bf16[512,4096]{1,0:T(8,128)(2,1)}, bf16[512,4096]{1,0:T(8,128)(2,1)}) fusion(f32[512,4096]{1,0:T(8,128)} %get-tuple-element.140, f32[512]{0:T(512)S(1)} %get-tuple-element.74, f32[512,4096]{1,0:T(8,128)} %copy-done.4, f32[512]{0:T(512)S(1)} %get-tuple-element.145, ...), kind=kLoop, calls=%fused_computation.9 | loop fusion | flops 48234496 | bytes 83922944 | tf_op jit(solution)/shard_map/while/body/eval_jaxpr/convert_element_type | solution.py:199
  558.0 11.5 %reduce-scatter.9.cloned.1.call-done = bf16[512,256]{0,1:T(8,128)(2,1)} async-done(((bf16[4096,256]{0,1:T(8,128)(2,1)}), bf16[512,256]{0,1:T(8,128)(2,1)}) %reduce-scatter.9.cloned.1.call-update) | async-done | bytes 262160 | tf_op jit(solution)/shard_map/reduce_scatter | solution.py:221
  572.8 10.0 convolution_convert_fusion.5
  591.0 10.1 convolution_convert_fusion.1
  601.3 10.1 convolution_convert_fusion.2
  611.4 10.3 convolution_convert_fusion
  625.4 17.5 %reduce-scatter.11.cloned.1.call-done = bf16[256,512]{1,0:T(8,128)(2,1)} async-done(((bf16[2048,512]{1,0:T(8,128)(2,1)}), bf16[256,512]{1,0:T(8,128)(2,1)}) %reduce-scatter.11.cloned.1.call-update) | async-done | bytes 262160 | tf_op jit(solution)/shard_map/reduce_scatter | solution.py:244
  644.7 30.1 %reduce-scatter.13.cloned.1.call-done = bf16[256,128]{1,0:T(8,128)(2,1)} async-done(((bf16[2048,128]{1,0:T(8,128)(2,1)}), bf16[256,128]{1,0:T(8,128)(2,1)}) %reduce-scatter.13.cloned.1.call-update) | async-done | bytes 65552 | tf_op jit(solution)/shard_map/reduce_scatter | solution.py:247
  676.2 30.1 %reduce-scatter.15.cloned.1.call-done = bf16[256,128]{1,0:T(8,128)(2,1)} async-done(((bf16[2048,128]{1,0:T(8,128)(2,1)}), bf16[256,128]{1,0:T(8,128)(2,1)}) %reduce-scatter.15.cloned.1.call-update) | async-done | bytes 65552 | tf_op jit(solution)/shard_map/reduce_scatter | solution.py:250
  707.8 105.0 %all-reduce.12.cloned.1.call-done = (bf16[512,2048]{1,0:T(8,128)(2,1)}, bf16[512,2048]{1,0:T(8,128)(2,1)}) async-done(((bf16[512,2048]{1,0:T(8,128)(2,1)}, bf16[512,2048]{1,0:T(8,128)(2,1)}), (bf16[512,2048]{1,0:T(8,128)(2,1)}, bf16[512,2048]{1,0:T(8,128)(2,1)})) %all-reduce.12.cloned.1.call-update) | async-done | bytes 4194320 | tf_op jit(solution)/shard_map/psum | solution.py:169
  816.0 17.4 %all-reduce.2 = (bf16[2048]{0:T(1024)(128)(2,1)S(1)}, bf16[2048]{0:T(1024)(128)(2,1)S(1)}) all-reduce(bf16[2048]{0:T(1024)(128)(2,1)S(1)} %get-tuple-element.67, bf16[2048]{0:T(1024)(128)(2,1)S(1)} %copy-done.52), channel_id=3, replica_groups=mesh['wide'=8,'narrow'=4] {'wide'}, use_global_device_ids=true, to_apply=%region_38.39.clone | all-reduce | flops 4096 | bytes 16384
  834.7 5.1 add_convert_fusion.2
  843.5 61.7 %reduce-scatter.21.cloned.1.call-done = bf16[256,2048]{1,0:T(8,128)(2,1)} async-done(((bf16[2048,2048]{1,0:T(8,128)(2,1)}), bf16[256,2048]{1,0:T(8,128)(2,1)}) %reduce-scatter.21.cloned.1.call-update) | async-done | bytes 1048592 | tf_op jit(solution)/shard_map/reduce_scatter | solution.py:262
  908.0 87.4 %reduce-scatter.19.cloned.1.call-done = bf16[256,2048]{1,0:T(8,128)(2,1)} async-done(((bf16[2048,2048]{1,0:T(8,128)(2,1)}), bf16[256,2048]{1,0:T(8,128)(2,1)}) %reduce-scatter.19.cloned.1.call-update) | async-done | bytes 1048592 | tf_op jit(solution)/shard_map/reduce_scatter | solution.py:259
  998.2 87.4 %reduce-scatter.23.cloned.1.call-done = bf16[2048,256]{1,0:T(8,128)(2,1)} async-done(((bf16[2048,2048]{1,0:T(8,128)(2,1)}), bf16[2048,256]{1,0:T(8,128)(2,1)}) %reduce-scatter.23.cloned.1.call-update) | async-done | bytes 1048592 | tf_op jit(solution)/shard_map/reduce_scatter | solution.py:265
  (313 shorter events, 210.1 us)
Async XLA Ops:
  7.2 123.9 %copy-start = (bf16[512,2048]{1,0:T(8,128)(2,1)S(1)}, bf16[512,2048]{1,0:T(8,128)(2,1)}, u32[]{:S(2)}) copy-start(bf16[512,2048]{1,0:T(8,128)(2,1)} %param.21) | copy-start | bytes 6291460
  7.2 7.9 copy-start.40
  7.2 42.6 %all-gather.2.cloned.1.call-start = ((), (), s32[]{:S(2)}) async-start(), calls=%async_computation.8 | async-start | bytes 2359296 | tf_op jit(solution)/shard_map/all_gather | solution.py:109
  10.1 9.4 copy-start.50
  17.9 220.0 %all-reduce.8.cloned.1.call-start = ((), (), s32[]{:S(2)}) async-start(), calls=%async_computation.9 | async-start | bytes 8388608 | tf_op jit(solution)/shard_map/psum | solution.py:150
  19.3 345.7 %copy-start.53 = (pred[512]{0:T(512)(128)(4,1)}, pred[512]{0:T(512)(128)(4,1)S(1)}, u32[]{:S(2)}) copy-start(pred[512]{0:T(512)(128)(4,1)S(1)} %fusion.150) | copy-start | bytes 1540
  61.6 64.6 %copy-start.4 = (f32[512,4096]{1,0:T(8,128)}, f32[512,4096]{1,0:T(8,128)S(1)}, u32[]{:S(2)}) copy-start(f32[512,4096]{1,0:T(8,128)S(1)} %get-tuple-element.136) | copy-start | bytes 25165828
  88.9 25.9 %copy-start.5 = (f32[512,4096]{1,0:T(8,128)}, f32[512,4096]{1,0:T(8,128)S(1)}, u32[]{:S(2)}) copy-start(f32[512,4096]{1,0:T(8,128)S(1)} %get-tuple-element.128) | copy-start | bytes 25165828
  94.7 18.3 %copy-start.6 = (f32[512,4096]{1,0:T(8,128)}, f32[512,4096]{1,0:T(8,128)S(1)}, u32[]{:S(2)}) copy-start(f32[512,4096]{1,0:T(8,128)S(1)} %get-tuple-element.126) | copy-start | bytes 25165828
  134.4 222.1 %all-reduce.10.cloned.1.call-start = ((), (), s32[]{:S(2)}) async-start(), calls=%async_computation.10 | async-start | bytes 4194304 | tf_op jit(solution)/shard_map/psum | solution.py:171
  241.4 9.8 copy-start.2
  241.4 9.8 slice-start.22
  241.8 9.4 copy-start.35
  241.8 9.4 slice-start.23
  286.7 282.8 %reduce-scatter.9.cloned.1.call-start = ((), (), s32[]{:S(2)}) async-start(), calls=%async_computation.11 | async-start | bytes 2359296 | tf_op jit(solution)/shard_map/reduce_scatter | solution.py:221
  356.5 10.7 slice-start.14
  370.2 8.7 slice-start.20
  376.2 8.4 slice-start
  467.0 23.3 %copy-start.34 = (bf16[512,8,2,32]{0,3,2,1:T(8,128)(2,1)S(1)}, bf16[512,8,2,32]{0,3,2,1:T(8,128)(2,1)}, u32[]{:S(2)}) copy-start(bf16[512,8,2,32]{0,3,2,1:T(8,128)(2,1)} %pad_maximum_fusion.1) | copy-start | bytes 1572868
  533.5 90.1 %reduce-scatter.17.cloned.1.call-start = ((), (), s32[]{:S(2)}) async-start(), calls=%async_computation.15 | async-start | bytes 2359296 | tf_op jit(solution)/shard_map/reduce_scatter | solution.py:253
  538.4 104.5 %reduce-scatter.11.cloned.1.call-start = ((), (), s32[]{:S(2)}) async-start(), calls=%async_computation.12 | async-start | bytes 2359296 | tf_op jit(solution)/shard_map/reduce_scatter | solution.py:244
  555.0 15.5 %copy-start.28 = (bf16[512,2048]{1,0:T(8,128)(2,1)S(1)}, bf16[512,2048]{1,0:T(8,128)(2,1)}, u32[]{:S(2)}) copy-start(bf16[512,2048]{1,0:T(8,128)(2,1)} %param.16) | copy-start | bytes 6291460
  557.9 116.8 %reduce-scatter.13.cloned.1.call-start = ((), (), s32[]{:S(2)}) async-start(), calls=%async_computation.13 | async-start | bytes 589824 | tf_op jit(solution)/shard_map/reduce_scatter | solution.py:247
  572.4 133.9 %reduce-scatter.15.cloned.1.call-start = ((), (), s32[]{:S(2)}) async-start(), calls=%async_computation.14 | async-start | bytes 589824 | tf_op jit(solution)/shard_map/reduce_scatter | solution.py:250
  572.8 10.1 copy-start.47
  584.7 228.1 %all-reduce.12.cloned.1.call-start = ((), (), s32[]{:S(2)}) async-start(), calls=%async_computation.19 | async-start | bytes 8388608 | tf_op jit(solution)/shard_map/psum | solution.py:169
  590.9 314.3 %reduce-scatter.21.cloned.1.call-start = ((), (), s32[]{:S(2)}) async-start(), calls=%async_computation.17 | async-start | bytes 9437184 | tf_op jit(solution)/shard_map/reduce_scatter | solution.py:262
  601.1 394.3 %reduce-scatter.19.cloned.1.call-start = ((), (), s32[]{:S(2)}) async-start(), calls=%async_computation.16 | async-start | bytes 9437184 | tf_op jit(solution)/shard_map/reduce_scatter | solution.py:259
  611.4 474.3 %reduce-scatter.23.cloned.1.call-start = ((), (), s32[]{:S(2)}) async-start(), calls=%async_computation.18 | async-start | bytes 9437184 | tf_op jit(solution)/shard_map/reduce_scatter | solution.py:265
  621.7 194.2 %copy-start.52 = (bf16[2048]{0:T(1024)(128)(2,1)S(1)}, bf16[2048]{0:T(1024)(128)(2,1)}, u32[]{:S(2)}) copy-start(bf16[2048]{0:T(1024)(128)(2,1)} %get-tuple-element.65) | copy-start | bytes 12292
  642.9 196.9 %copy-start.55 = (f32[512]{0:T(512)S(1)}, f32[512]{0:T(512)}, u32[]{:S(2)}) copy-start(f32[512]{0:T(512)} %get-tuple-element.119) | copy-start | bytes 6148
  840.9 247.5 %copy-start.1 = (bf16[512,2048]{1,0:T(8,128)(2,1)S(1)}, bf16[512,2048]{1,0:T(8,128)(2,1)}, u32[]{:S(2)}) copy-start(bf16[512,2048]{1,0:T(8,128)(2,1)} %param.21) | copy-start | bytes 6291460
  (64 other events, 237.7 us)
Sparse Core Ops, SparseCore 0:
  18.0 31.7 all-gather.1
  134.5 103.3 all-reduce.7
  286.8 69.6 all-reduce.9
  533.6 35.8 reduce-scatter.8
  571.6 34.4 reduce-scatter.16
  608.3 34.5 reduce-scatter.10
  645.1 29.5 reduce-scatter.12
  677.1 29.1 reduce-scatter.14
  710.4 102.3 all-reduce.11
  815.0 90.1 reduce-scatter.20
  907.6 87.7 reduce-scatter.18
  997.7 87.9 reduce-scatter.22
where the time goes:
time: 1100 us
  waiting for transfers between devices  629 us (57%)
  matrix products  293 us (27%)
  other arithmetic  112 us (10%)
  local copies, waits for them, and re-layouts  25.3 us (2%)
  blocking collectives  17.4 us (2%)
  between operations  16.3 us (1%)
    dot_general x23, matrix products, contract_cols(): lax.dot_general(left, right, (((1,), (1,)), ((), ())), preferred_element_...  147 us
    psum x1, waiting for transfers between devices, body(): lax.psum(ffn_part.astype(jnp.bfloat16), 'narrow').astype(jnp.float32)  105 us
    psum x1, waiting for transfers between devices, body(): hidden_one = inputs + lax.psum(attn_part, 'narrow')  103 us
    reduce_scatter x1, waiting for transfers between devices, body(): lax.psum_scatter(grad_down.astype(jnp.bfloat16), 'wide', scatter_dimensio...  87.4 us
    reduce_scatter x1, waiting for transfers between devices, body(): lax.psum_scatter(grad_gate.astype(jnp.bfloat16), 'wide', scatter_dimensio...  87.4 us
    dot_general x23, matrix products, contract_rows(): lax.dot_general(left, right, (((0,), (0,)), ((), ())), preferred_element_...  73.2 us
    psum x1, waiting for transfers between devices, body(): lax.psum(norm_two_part.astype(jnp.bfloat16), 'narrow').astype(jnp.float32)  69.3 us
    reduce_scatter x1, waiting for transfers between devices, body(): lax.psum_scatter(grad_up.astype(jnp.bfloat16), 'wide', scatter_dimension=...  61.7 us
  transfers between devices with their start and end apart: 12, of which 11 were waited for; matrix products, arithmetic and copies ran while one was open for 10% of the time, Pallas kernels for 0%

commit v1 on v0

--- a/solution.py
+++ b/solution.py
@@ -1,15 +1,36 @@
+import functools
 import math
 import jax
 import jax.numpy as jnp
 import numpy as np
 from jax import lax
 from jax.sharding import PartitionSpec as P
+from jax.lax import axis_index, ppermute, psum
 
 HD = 64
 QBLK = 512
 DOCS = 12
 NORM_EPS = 1e-05
 MASKED_SCORE = -1e30
+
+
+def cover_map(my_tile, shard_axis, axis_no):
+    total_devices = psum(1, shard_axis)
+    table = []
+    for dev_i in range(1, total_devices):
+        table.append((dev_i - 1, dev_i))
+    extra = table + [(total_devices - 1, 0)]
+    back = my_tile
+    frames = [back]
+    for _ in range(total_devices - 1):
+        back = ppermute(back, shard_axis, extra)
+        frames += [back]
+    seen_now = jnp.concatenate([*reversed(frames)], axis=axis_no)
+    local_out = axis_index(shard_axis)
+    return jnp.roll(seen_now, (local_out + 1) * back.shape[axis_no], axis=axis_no)
+
+
+sheets_balance = functools.partial(cover_map, shard_axis="wide", axis_no=0)
 
 
 def inverse_frequencies(head_size):
@@ -106,7 +127,7 @@
     query_r = rotate(query, position, heads, 1.0).astype(jnp.bfloat16)
     keys_r = rotate(keys, position, kv_heads, 1.0).astype(jnp.bfloat16)
     packed = jnp.concatenate([keys_r, values], axis=1)
-    gathered = lax.all_gather(packed, "wide", axis=0, tiled=True)
+    gathered = sheets_balance(packed)
     width = kv_heads * HD
     all_keys = gathered[:, :width]
     all_values = gathered[:, width:]

time: 1100 us -> 1140 us (1.036)
  waiting for transfers between devices: 629 us -> 651 us
  other arithmetic: 112 us -> 129 us
    ppermute x0 -> x7, waiting for transfers between devices: none -> 48.6 us  [cover_map(): back = ppermute(back, shard_axis, extra)]
    all_gather x1 -> x0, waiting for transfers between devices: 25.7 us -> none  [body(): gathered = lax.all_gather(packed, 'wide', axis=0, tiled=True)]
    reduce_sum x8, other arithmetic: 13.9 us -> 30.4 us  [attend(): row_sum = jnp.sum(exponent, axis=1, keepdims=True)]
    unnamed x169 -> x207, local copies, waits for them, and re-layouts: 23.8 us -> 21 us
  transfers between devices with their start and end apart: 12 -> 18, of which waited for: 11 -> 17; matrix products, arithmetic and copies ran while one was open for 10% -> 9% of each run, Pallas kernels for 0% -> 0%
where the time goes in v1:
time: 1140 us; the launch traced here: 1130 us
  waiting for transfers between devices  651 us (57%)
  matrix products  294 us (26%)
  other arithmetic  129 us (11%)
  local copies, waits for them, and re-layouts  22.5 us (2%)
  blocking collectives  17.2 us (2%)
  between operations  16.4 us (1%)
    dot_general x23, matrix products, contract_cols(): lax.dot_general(left, right, (((1,), (1,)), ((), ())), preferred_element_...  151 us
    psum x1, waiting for transfers between devices, body(): lax.psum(ffn_part.astype(jnp.bfloat16), 'narrow').astype(jnp.float32)  105 us
    psum x1, waiting for transfers between devices, body(): hidden_one = inputs + lax.psum(attn_part, 'narrow')  103 us
    reduce_scatter x1, waiting for transfers between devices, body(): lax.psum_scatter(grad_down.astype(jnp.bfloat16), 'wide', scatter_dimensio...  87.6 us
    reduce_scatter x1, waiting for transfers between devices, body(): lax.psum_scatter(grad_gate.astype(jnp.bfloat16), 'wide', scatter_dimensio...  87.3 us
    dot_general x23, matrix products, contract_rows(): lax.dot_general(left, right, (((0,), (0,)), ((), ())), preferred_element_...  76 us
    psum x1, waiting for transfers between devices, body(): lax.psum(norm_two_part.astype(jnp.bfloat16), 'narrow').astype(jnp.float32)  69.4 us
    reduce_scatter x1, waiting for transfers between devices, body(): lax.psum_scatter(grad_up.astype(jnp.bfloat16), 'wide', scatter_dimension=...  62.1 us
  transfers between devices with their start and end apart: 18, of which 17 were waited for; matrix products, arithmetic and copies ran while one was open for 9% of the time, Pallas kernels for 0%

profile of v1, /device:TPU:0, one launch (start us, length us, event | category | flops | bytes accessed | tf_op | source)
XLA Modules:
  0.0 1133.2 jit_solution(17906079457685394254)
XLA Ops:
  17.9 8.1 collective-permute-done
  26.0 7.6 collective-permute-done.1
  33.6 7.6 collective-permute-done.2
  41.2 7.6 collective-permute-done.3
  48.8 7.6 collective-permute-done.4
  67.0 5.5 collective-permute-done.6
  110.2 7.7 fusion.6
  165.5 102.6 %all-reduce.8.cloned.1.call-done = f32[512,2048]{1,0:T(8,128)} async-done(((f32[512,2048]{1,0:T(8,128)}), f32[512,2048]{1,0:T(8,128)}) %all-reduce.8.cloned.1.call-update) | async-done | bytes 4194320 | tf_op jit(solution)/shard_map/psum | solution.py:171
  272.1 9.3 fusion.186
  281.5 6.3 fusion.185
  287.8 12.0 %multiply_convert_fusion.8 = (bf16[512,2048]{1,0:T(8,128)(2,1)}, bf16[512,2048]{1,0:T(8,128)(2,1)}, bf16[512,2048]{1,0:T(8,128)(2,1)}) fusion(f32[512,2048]{1,0:T(8,128)} %fusion.185, f32[512,2048]{1,0:T(8,128)S(1)} %fusion.186, bf16[512,2048]{1,0:T(8,128)(2,1)S(1)} %copy-done.35, bf16[2048,2048]{1,0:T(8,128)(2,1)} %param.25), kind=kOutput, calls=%fused_computation.118 | convolution fusion | flops 4310695936 | bytes 25165824 | tf_op jit(solution)/shard_map/dot_general | solution.py:77
  299.8 7.8 fusion.187
  307.6 9.4 add_convert_fusion.1
  317.4 69.4 %all-reduce.10.cloned.1.call-done = bf16[512,2048]{1,0:T(8,128)(2,1)} async-done(((bf16[512,2048]{1,0:T(8,128)(2,1)}), bf16[512,2048]{1,0:T(8,128)(2,1)}) %all-reduce.10.cloned.1.call-update) | async-done | bytes 2097168 | tf_op jit(solution)/shard_map/psum | solution.py:192
  421.2 5.5 fusion.108
  452.0 27.3 %multiply_reduce_fusion = (f32[512]{0:T(512)S(1)}, f32[512]{0:T(512)S(1)}, f32[512]{0:T(512)S(1)}, f32[512]{0:T(512)S(1)}, f32[512]{0:T(512)S(1)}, /*index=5*/f32[512,4096]{1,0:T(8,128)}) fusion(f32[512,4096]{1,0:T(8,128)} %get-tuple-element.138, f32[512]{0:T(512)S(1)} %log_add_fusion, s32[512]{0:T(512)S(1)} %copy-done.52, s32[4096]{0:T(1024)S(1)} %copy-done.49, ...), kind=kOutput, calls=%fused_computation.7 | convolution fusion | flops 316667392 | bytes 84516872 | tf_op jit(solution)/shard_map/while/body/eval_jaxpr/dot_general | solution.py:77
  479.3 26.9 %multiply_reduce_fusion.1 = (f32[512]{0:T(512)S(1)}, f32[512]{0:T(512)S(1)}, f32[512]{0:T(512)S(1)}, bf16[512,4096]{1,0:T(8,128)(2,1)}, f32[512,4096]{1,0:T(8,128)}) fusion(f32[512,4096]{1,0:T(8,128)} %get-tuple-element.136, f32[512]{0:T(512)S(1)} %get-tuple-element.145, s32[512]{0:T(512)S(1)} %copy-done.52, s32[4096]{0:T(1024)S(1)} %copy-done.49, ...), kind=kOutput, calls=%fused_computation.10 | convolution fusion | flops 310376960 | bytes 71929864 | tf_op jit(solution)/shard_map/while/body/eval_jaxpr/dot_general | solution.py:77
  506.2 21.4 %multiply_convert_fusion.2 = (bf16[512,4096]{1,0:T(8,128)(2,1)}, bf16[512,4096]{1,0:T(8,128)(2,1)}, bf16[512,4096]{1,0:T(8,128)(2,1)S(1)}) fusion(f32[512,4096]{1,0:T(8,128)} %fusion.86, f32[512]{0:T(512)S(1)} %get-tuple-element.88, f32[512,4096]{1,0:T(8,128)} %get-tuple-element.134, f32[512]{0:T(512)S(1)} %get-tuple-element.146, s32[512]{0:T(512)S(1)} %copy-done.52, ...), kind=kLoop, calls=%fused_computation.12 | loop fusion | flops 37748736 | bytes 62947328 | tf_op jit(solution)/shard_map/while/body/eval_jaxpr/convert_element_type | solution.py:220
  530.5 26.9 %multiply_convert_fusion.1 = (bf16[512,4096]{1,0:T(8,128)(2,1)}, bf16[512,4096]{1,0:T(8,128)(2,1)}, bf16[512,4096]{1,0:T(8,128)(2,1)}, bf16[512,4096]{1,0:T(8,128)(2,1)}) fusion(f32[512,4096]{1,0:T(8,128)} %get-tuple-element.140, f32[512]{0:T(512)S(1)} %get-tuple-element.74, f32[512,4096]{1,0:T(8,128)} %get-tuple-element.136, f32[512]{0:T(512)S(1)} %get-tuple-element.145, ...), kind=kLoop, calls=%fused_computation.9 | loop fusion | flops 48234496 | bytes 83922944 | tf_op jit(solution)/shard_map/while/body/eval_jaxpr/convert_element_type | solution.py:220
  596.6 11.1 reduce-scatter.9.cloned.1.call-done
  610.8 10.0 convolution_convert_fusion.5
  628.9 10.1 convolution_convert_fusion.1
  639.3 10.1 convolution_convert_fusion.2
  649.5 10.3 convolution_convert_fusion
  663.5 17.2 %reduce-scatter.11.cloned.1.call-done = bf16[256,512]{1,0:T(8,128)(2,1)} async-done(((bf16[2048,512]{1,0:T(8,128)(2,1)}), bf16[256,512]{1,0:T(8,128)(2,1)}) %reduce-scatter.11.cloned.1.call-update) | async-done | bytes 262160 | tf_op jit(solution)/shard_map/reduce_scatter | solution.py:265
  682.4 30.1 %reduce-scatter.13.cloned.1.call-done = bf16[256,128]{1,0:T(8,128)(2,1)} async-done(((bf16[2048,128]{1,0:T(8,128)(2,1)}), bf16[256,128]{1,0:T(8,128)(2,1)}) %reduce-scatter.13.cloned.1.call-update) | async-done | bytes 65552 | tf_op jit(solution)/shard_map/reduce_scatter | solution.py:268
  714.0 30.0 %reduce-scatter.15.cloned.1.call-done = bf16[256,128]{1,0:T(8,128)(2,1)} async-done(((bf16[2048,128]{1,0:T(8,128)(2,1)}), bf16[256,128]{1,0:T(8,128)(2,1)}) %reduce-scatter.15.cloned.1.call-update) | async-done | bytes 65552 | tf_op jit(solution)/shard_map/reduce_scatter | solution.py:271
  745.5 105.1 %all-reduce.12.cloned.1.call-done = (bf16[512,2048]{1,0:T(8,128)(2,1)}, bf16[512,2048]{1,0:T(8,128)(2,1)}) async-done(((bf16[512,2048]{1,0:T(8,128)(2,1)}, bf16[512,2048]{1,0:T(8,128)(2,1)}), (bf16[512,2048]{1,0:T(8,128)(2,1)}, bf16[512,2048]{1,0:T(8,128)(2,1)})) %all-reduce.12.cloned.1.call-update) | async-done | bytes 4194320 | tf_op jit(solution)/shard_map/psum | solution.py:190
  853.8 17.2 %all-reduce.2 = (bf16[2048]{0:T(1024)(128)(2,1)S(1)}, bf16[2048]{0:T(1024)(128)(2,1)S(1)}) all-reduce(bf16[2048]{0:T(1024)(128)(2,1)S(1)} %get-tuple-element.67, bf16[2048]{0:T(1024)(128)(2,1)S(1)} %copy-done.59), channel_id=3, replica_groups=mesh['wide'=8,'narrow'=4] {'wide'}, use_global_device_ids=true, to_apply=%region_38.39.clone | all-reduce | flops 4096 | bytes 16384
  881.1 62.1 %reduce-scatter.21.cloned.1.call-done = bf16[256,2048]{1,0:T(8,128)(2,1)} async-done(((bf16[2048,2048]{1,0:T(8,128)(2,1)}), bf16[256,2048]{1,0:T(8,128)(2,1)}) %reduce-scatter.21.cloned.1.call-update) | async-done | bytes 1048592 | tf_op jit(solution)/shard_map/reduce_scatter | solution.py:283
  946.0 87.3 %reduce-scatter.19.cloned.1.call-done = bf16[256,2048]{1,0:T(8,128)(2,1)} async-done(((bf16[2048,2048]{1,0:T(8,128)(2,1)}), bf16[256,2048]{1,0:T(8,128)(2,1)}) %reduce-scatter.19.cloned.1.call-update) | async-done | bytes 1048592 | tf_op jit(solution)/shard_map/reduce_scatter | solution.py:280
  1036.1 87.6 %reduce-scatter.23.cloned.1.call-done = bf16[2048,256]{1,0:T(8,128)(2,1)} async-done(((bf16[2048,2048]{1,0:T(8,128)(2,1)}), bf16[2048,256]{1,0:T(8,128)(2,1)}) %reduce-scatter.23.cloned.1.call-update) | async-done | bytes 1048592 | tf_op jit(solution)/shard_map/reduce_scatter | solution.py:286
  (365 shorter events, 252.3 us)
Async XLA Ops:
  7.2 154.8 %copy-start = (bf16[512,2048]{1,0:T(8,128)(2,1)S(1)}, bf16[512,2048]{1,0:T(8,128)(2,1)}, u32[]{:S(2)}) copy-start(bf16[512,2048]{1,0:T(8,128)(2,1)} %param.21) | copy-start | bytes 6291460
  7.2 260.9 %all-reduce.8.cloned.1.call-start = ((), (), s32[]{:S(2)}) async-start(), calls=%async_computation.8 | async-start | bytes 8388608 | tf_op jit(solution)/shard_map/psum | solution.py:171
  7.3 100.3 %copy-start.51 = (s32[512]{0:T(512)}, s32[512]{0:T(512)S(1)}, u32[]{:S(2)}) copy-start(s32[512]{0:T(512)S(1)} %iota_add_fusion) | copy-start | bytes 6148
  10.2 46.2 %copy-start.57 = (f32[512]{0:T(512)}, f32[512]{0:T(512)S(1)}, u32[]{:S(2)}) copy-start(f32[512]{0:T(512)S(1)} %get-tuple-element.120) | copy-start | bytes 6148
  11.9 95.7 %copy-start.55 = (s32[512]{0:T(512)}, s32[512]{0:T(512)S(1)}, u32[]{:S(2)}) copy-start(s32[512]{0:T(512)S(1)} %get-tuple-element.89) | copy-start | bytes 6148
  12.6 43.8 %copy-start.53 = (f32[2048]{0:T(1024)}, f32[2048]{0:T(1024)S(1)}, u32[]{:S(2)}) copy-start(f32[2048]{0:T(1024)S(1)} %convert_element_type.251) | copy-start | bytes 24580
  12.6 43.8 %copy-start.34 = (bf16[2048,512]{1,0:T(8,128)(2,1)S(1)}, bf16[2048,512]{1,0:T(8,128)(2,1)}, u32[]{:S(2)}) copy-start(bf16[2048,512]{1,0:T(8,128)(2,1)} %param.18) | copy-start | bytes 6291460
  17.3 41.2 %copy-start.36 = (f32[512,32]{0,1:T(8,128)}, f32[512,32]{0,1:T(8,128)S(1)}, u32[]{:S(2)}) copy-start(f32[512,32]{0,1:T(8,128)S(1)} %get-tuple-element.118) | copy-start | bytes 196612
  17.4 8.6 collective-permute-start
  26.0 7.6 collective-permute-start.1
  33.6 7.6 collective-permute-start.2
  41.2 7.6 collective-permute-start.3
  48.8 7.6 collective-permute-start.4
  56.3 7.7 collective-permute-start.5
  64.0 8.4 collective-permute-start.6
  65.9 41.8 %copy-start.48 = (s32[4096]{0:T(1024)}, s32[4096]{0:T(1024)S(1)}, u32[]{:S(2)}) copy-start(s32[4096]{0:T(1024)S(1)} %convert_reduce_fusion) | copy-start | bytes 49156
  67.0 40.7 %copy-start.31 = (bf16[512,8,2,32]{0,3,2,1:T(8,128)(2,1)}, bf16[512,8,2,32]{0,3,2,1:T(8,128)(2,1)S(1)}, u32[]{:S(2)}) copy-start(bf16[512,8,2,32]{0,3,2,1:T(8,128)(2,1)S(1)} %pad_maximum_fusion.1) | copy-start | bytes 1572868
  94.7 48.8 %copy-start.4 = (f32[512,4096]{1,0:T(8,128)}, f32[512,4096]{1,0:T(8,128)S(1)}, u32[]{:S(2)}) copy-start(f32[512,4096]{1,0:T(8,128)S(1)} %get-tuple-element.126) | copy-start | bytes 25165828
  97.3 49.3 %copy-start.5 = (f32[512,4096]{1,0:T(8,128)}, f32[512,4096]{1,0:T(8,128)S(1)}, u32[]{:S(2)}) copy-start(f32[512,4096]{1,0:T(8,128)S(1)} %get-tuple-element.128) | copy-start | bytes 25165828
  165.4 221.4 %all-reduce.10.cloned.1.call-start = ((), (), s32[]{:S(2)}) async-start(), calls=%async_computation.9 | async-start | bytes 4194304 | tf_op jit(solution)/shard_map/psum | solution.py:192
  317.0 290.6 %reduce-scatter.9.cloned.1.call-start = ((), (), s32[]{:S(2)}) async-start(), calls=%async_computation.10 | async-start | bytes 2359296 | tf_op jit(solution)/shard_map/reduce_scatter | solution.py:242
  571.7 90.0 %reduce-scatter.17.cloned.1.call-start = ((), (), s32[]{:S(2)}) async-start(), calls=%async_computation.14 | async-start | bytes 2359296 | tf_op jit(solution)/shard_map/reduce_scatter | solution.py:274
  576.6 104.1 %reduce-scatter.11.cloned.1.call-start = ((), (), s32[]{:S(2)}) async-start(), calls=%async_computation.11 | async-start | bytes 2359296 | tf_op jit(solution)/shard_map/reduce_scatter | solution.py:265
  596.5 116.0 %reduce-scatter.13.cloned.1.call-start = ((), (), s32[]{:S(2)}) async-start(), calls=%async_computation.12 | async-start | bytes 589824 | tf_op jit(solution)/shard_map/reduce_scatter | solution.py:268
  610.6 133.5 %reduce-scatter.15.cloned.1.call-start = ((), (), s32[]{:S(2)}) async-start(), calls=%async_computation.13 | async-start | bytes 589824 | tf_op jit(solution)/shard_map/reduce_scatter | solution.py:271
  622.7 227.9 %all-reduce.12.cloned.1.call-start = ((), (), s32[]{:S(2)}) async-start(), calls=%async_computation.18 | async-start | bytes 8388608 | tf_op jit(solution)/shard_map/psum | solution.py:190
  628.9 314.3 %reduce-scatter.21.cloned.1.call-start = ((), (), s32[]{:S(2)}) async-start(), calls=%async_computation.16 | async-start | bytes 9437184 | tf_op jit(solution)/shard_map/reduce_scatter | solution.py:283
  639.1 394.2 %reduce-scatter.19.cloned.1.call-start = ((), (), s32[]{:S(2)}) async-start(), calls=%async_computation.15 | async-start | bytes 9437184 | tf_op jit(solution)/shard_map/reduce_scatter | solution.py:280
  649.5 474.2 %reduce-scatter.23.cloned.1.call-start = ((), (), s32[]{:S(2)}) async-start(), calls=%async_computation.17 | async-start | bytes 9437184 | tf_op jit(solution)/shard_map/reduce_scatter | solution.py:286
  659.8 194.0 %copy-start.59 = (bf16[2048]{0:T(1024)(128)(2,1)S(1)}, bf16[2048]{0:T(1024)(128)(2,1)}, u32[]{:S(2)}) copy-start(bf16[2048]{0:T(1024)(128)(2,1)} %get-tuple-element.65) | copy-start | bytes 12292
  680.6 196.7 %copy-start.61 = (f32[512]{0:T(512)S(1)}, f32[512]{0:T(512)}, u32[]{:S(2)}) copy-start(f32[512]{0:T(512)} %get-tuple-element.119) | copy-start | bytes 6148
  878.5 247.9 %copy-start.1 = (bf16[512,2048]{1,0:T(8,128)(2,1)S(1)}, bf16[512,2048]{1,0:T(8,128)(2,1)}, u32[]{:S(2)}) copy-start(bf16[512,2048]{1,0:T(8,128)(2,1)} %param.21) | copy-start | bytes 6291460
  (82 other events, 485.6 us)
Sparse Core Ops, SparseCore 0:
  165.6 102.5 all-reduce.7
  317.1 69.6 all-reduce.9
  571.8 35.7 reduce-scatter.8
  609.8 34.3 reduce-scatter.16
  646.3 34.2 reduce-scatter.10
  682.7 29.7 reduce-scatter.12
  714.9 29.1 reduce-scatter.14
  748.1 102.4 all-reduce.11
  853.0 90.1 reduce-scatter.20
  945.4 87.7 reduce-scatter.18
  1035.7 87.9 reduce-scatter.22
